TPU v7x, 128 devices: a whole 4x4x4 slice. The times are simulated.
128 devices in a mesh: slab: 16 (over x, z), chan: 8 (over y, core).
Axes of the slice: x: 4, y: 4, z: 4, core: 2. Of those that a mesh axis runs over, the one named last changes fastest.
Arguments:
- stream_speed_field: bfloat16 [3, 8, 8, 8, 65536], P(None, None, None, None, ('slab', 'chan')), may hold values from -6 to 6
- liquid_to_solid_element: int32 [65536], P(('slab', 'chan')), may hold values from 0 to 65535, as said below
- previous_panel_warmth: float32 [8, 8, 8, 16, 4096], P(None, None, None, 'chan', 'slab'), may hold values from -6 to 6
- pointwise_energy_source: float32 [8, 8, 8, 16, 4096], P(None, None, None, 'chan', 'slab'), may hold values from -6 to 6
- coked_element_flags: int32 [16, 4096], P('chan', 'slab'), may hold values from 0 to 1, as said below
- coking_thickness_plies: int32 [16, 4096], P('chan', 'slab'), may hold values from 1 to 8
Outputs:
- stepped_stream_speed: bfloat16 [3, 8, 8, 8, 65536], P(None, None, None, None, ('slab', 'chan'))
- solved_panel_warmth: float32 [8, 8, 8, 16, 4096], P(None, None, None, 'chan', 'slab')
Inputs may be any that keep to these rules, and one draw needn't show every extreme that they name: `liquid_to_solid_element`: A permutation of the element numbers. Element n belongs to thermal device n // 512 (devices numbered slab first, then chan) at local position n % 512. The fluid device f holds 256 elements of thermal device f and at most 128 of each of the thermal devices f + 1, f - 1 and f + 8 (modulo the number of devices), none of any other; these three counts are the same for every f, and one of them is 128. `coked_element_flags`: at most 192 flagged elements among one thermal device's elements, and exactly 192 on some device.
All inputs are finite; a program needn't handle non-finite values.
Results may differ from a plain program's by a relative error of at most 0.005.
Values may be sent and summed in bfloat16 or wider, within the bound.
A program may use at most 128 MiB of HBM per device.

v0:
```python
import jax
import jax.numpy as jnp
import numpy as np
from jax import lax
from jax.sharding import PartitionSpec as P

ITERS = 5


highest = lax.Precision.HIGHEST
coolant_throughput = 0.05
time_step = 0.01
viscosity = 0.02
cross_gain = 0.4
layer_damp = 0.25
forward_forms = ("ir,rst...->ist...", "js,rst...->rjt...", "kt,rst...->rsk...")
backward_forms = ("ir,ist...->rst...", "js,rjt...->rst...", "kt,rsk...->rst...")
fluid_forms = ("ir,crste->ciste", "js,crste->crjte", "kt,crste->crske")


def from_behind(block, axis, distance):
    devices = range(lax.axis_size(axis))
    route = [((i - distance) % len(devices), i) for i in devices]
    return lax.ppermute(block, axis, route)


def with_halo(x, sides, width):
    for axis, dim in sides:
        devices, length = (lax.axis_size(axis), x.shape[dim])
        up = [(i, (i + 1) % devices) for i in range(devices - 1)]
        down = [(j, i) for i, j in up]
        last = lax.slice_in_dim(x, length - width, length, axis=dim)
        initial = lax.slice_in_dim(x, 0, width, axis=dim)
        before = lax.ppermute(last, axis, up)
        after = lax.ppermute(initial, axis, down)
        x = jnp.concatenate([before, x, after], axis=dim)
    return x


def gll_tables():
    points = np.array(
        [
            -1.0,
            -0.8717401485096066,
            -0.5917001814331423,
            -0.2092992179024789,
            0.2092992179024789,
            0.5917001814331423,
            0.8717401485096066,
            1.0,
        ]
    )
    weights = np.array(
        [
            1.0 / 28.0,
            0.2107042271435061,
            0.3411226924835044,
            0.4124587946587038,
            0.4124587946587038,
            0.3411226924835044,
            0.2107042271435061,
            1.0 / 28.0,
        ]
    )
    lower_poly = np.ones(8)
    upper_poly = points.copy()
    for degree in range(1, 7):
        next_poly = ((2 * degree + 1) * points * upper_poly - degree * lower_poly) / (degree + 1)
        lower_poly = upper_poly
        upper_poly = next_poly
    gaps_matrix = points[:, None] - points[None, :] + np.eye(8)
    derivative = upper_poly[:, None] / (upper_poly[None, :] * gaps_matrix)
    derivative = derivative * (1.0 - np.eye(8))
    derivative[0, 0] = -14.0
    derivative[7, 7] = 14.0
    return (jnp.asarray(derivative, jnp.float32), jnp.asarray(weights, jnp.float32))


def forward(matrix, field, conjugate_update_vector):
    return jnp.einsum(forward_forms[conjugate_update_vector], matrix, field, precision=highest)


def backward(matrix, field, conjugate_update_vector):
    return jnp.einsum(backward_forms[conjugate_update_vector], matrix, field, precision=highest)


def fluid_update(velocity_block, matrix):
    velocity_now = velocity_block.astype(jnp.float32)
    gradients = [
        jnp.einsum(fluid_forms[conjugate_update_vector], matrix, velocity_now, precision=highest)
        for conjugate_update_vector in range(3)
    ]
    convect = (
        velocity_now[0:1] * gradients[0]
        + velocity_now[1:2] * gradients[1]
        + velocity_now[2:3] * gradients[2]
    )
    laplace = jnp.einsum(fluid_forms[0], matrix, gradients[0], precision=highest)
    laplace = laplace + jnp.einsum(fluid_forms[1], matrix, gradients[1], precision=highest)
    laplace = laplace + jnp.einsum(fluid_forms[2], matrix, gradients[2], precision=highest)
    updated = velocity_now + time_step * (viscosity * laplace - convect)
    return updated.astype(jnp.bfloat16)


def conductivity_of(stepped_stream_speed):
    faster = stepped_stream_speed.astype(jnp.float32)
    return (
        1.0 + 0.5 * (faster[0] * faster[0] + faster[1] * faster[1] + faster[2] * faster[2])
    ).astype(jnp.bfloat16)


def move_blocks(payload, liquid_to_solid_element):
    row_count, element_count = payload.shape
    kept_count = element_count // 2
    capacity = element_count // 4
    chan_count = lax.axis_size("chan")
    device_total = lax.axis_size("slab") * chan_count
    my_device = lax.axis_index("slab") * chan_count + lax.axis_index("chan")
    target_dev = liquid_to_solid_element // element_count
    target_slot = liquid_to_solid_element % element_count
    distance = (target_dev - my_device) % device_total
    offset_group = jnp.where(
        distance == 1,
        1,
        jnp.where(distance == device_total - 1, 2, jnp.where(distance == chan_count, 3, 0)),
    ).astype(jnp.int32)
    onehot = (offset_group[:, None] == jnp.arange(4, dtype=jnp.int32)[None, :]).astype(jnp.int32)
    running = jnp.cumsum(onehot, axis=0) - 1
    slot_rank = jnp.sum(onehot * running, axis=1)
    starts = jnp.array([0, kept_count, kept_count + capacity, kept_count + 2 * capacity], jnp.int32)
    position = jnp.sum(onehot * starts[None, :], axis=1) + slot_rank
    code_high = (target_slot // 32).astype(jnp.bfloat16)
    code_low = (target_slot % 32).astype(jnp.bfloat16)
    tagged = jnp.concatenate([payload, code_high[None, :], code_low[None, :]], 0)
    buffer_width = kept_count + 3 * capacity
    blank = jnp.concatenate(
        [
            jnp.zeros((row_count, buffer_width), jnp.bfloat16),
            jnp.full((1, buffer_width), element_count // 32, jnp.bfloat16),
            jnp.full((1, buffer_width), element_count % 32, jnp.bfloat16),
        ],
        0,
    )
    packed = blank.at[:, position].set(tagged)
    collected = [packed[:, :kept_count]]
    outgoing_list = [
        packed[:, kept_count + number * capacity : kept_count + (number + 1) * capacity]
        for number in range(3)
    ]
    for number, offset_step in enumerate((1, -1, chan_count)):
        collected.append(from_behind(outgoing_list[number], ("slab", "chan"), offset_step))
    combined = jnp.concatenate(collected, 1)
    slot_index = combined[row_count].astype(jnp.int32) * 32 + combined[row_count + 1].astype(
        jnp.int32
    )
    return (
        jnp.zeros((row_count, element_count), jnp.bfloat16)
        .at[:, slot_index]
        .set(combined[:row_count], mode="drop")
    )


def gather_nodes(field):
    end_faces = jnp.stack([field[0, :, :, :, 0], field[7, :, :, :, -1]])
    with_rims = with_halo(end_faces, (("slab", 0),), 1)
    shared = field[7, :, :, :, :-1] + field[0, :, :, :, 1:]
    field = field.at[7, :, :, :, :-1].set(shared).at[0, :, :, :, 1:].set(shared)
    field = field.at[0, :, :, :, 0].add(with_rims[0]).at[7, :, :, :, -1].add(with_rims[3])
    side_faces = jnp.stack([field[:, 0, :, 0, :], field[:, 7, :, -1, :]])
    side_rims = with_halo(side_faces, (("chan", 0),), 1)
    shared = field[:, 7, :, :-1, :] + field[:, 0, :, 1:, :]
    field = field.at[:, 7, :, :-1, :].set(shared).at[:, 0, :, 1:, :].set(shared)
    field = field.at[:, 0, :, 0, :].add(side_rims[0]).at[:, 7, :, -1, :].add(side_rims[3])
    return field


def multiplicity(count_l, count_a, first_l, first_a, total_l, total_a):
    node_index = jnp.arange(8, dtype=jnp.int32)
    axial_pos = first_a + jnp.arange(count_a, dtype=jnp.int32)
    lateral_pos = first_l + jnp.arange(count_l, dtype=jnp.int32)
    along_axial = (
        1
        + ((node_index[:, None] == 0) & (axial_pos[None, :] > 0)).astype(jnp.int32)
        + ((node_index[:, None] == 7) & (axial_pos[None, :] < total_a - 1)).astype(jnp.int32)
    )
    along_lateral = (
        1
        + ((node_index[:, None] == 0) & (lateral_pos[None, :] > 0)).astype(jnp.int32)
        + ((node_index[:, None] == 7) & (lateral_pos[None, :] < total_l - 1)).astype(jnp.int32)
    )
    return (along_axial[:, None, None, None, :] * along_lateral[None, :, None, :, None]).astype(
        jnp.float32
    )


def on_device(
    stream_speed_field,
    liquid_to_solid_element,
    previous_panel_warmth,
    pointwise_energy_source,
    coked_element_flags,
    coking_thickness_plies,
):
    matrix, node_gll = gll_tables()
    integration_factor = (
        node_gll[:, None, None] * node_gll[None, :, None] * node_gll[None, None, :]
    )[:, :, :, None, None]
    count_l, count_a = coked_element_flags.shape
    element_count = count_l * count_a
    stepped_stream_speed = fluid_update(stream_speed_field, matrix)
    moved = move_blocks(
        conductivity_of(stepped_stream_speed).reshape(512, element_count), liquid_to_solid_element
    )
    moved = moved.reshape(8, 8, 8, count_l, count_a)
    layer_float = coking_thickness_plies.astype(jnp.float32)
    flag_float = coked_element_flags.astype(jnp.float32)
    damping = jnp.where(
        coked_element_flags == 1, 1.0 / (1.0 + layer_damp * layer_float), jnp.ones_like(layer_float)
    )
    weighted_kappa = integration_factor * (moved.astype(jnp.float32) * damping)
    cross_el = cross_gain * flag_float * layer_float / (layer_float + 1.0)
    first_a = lax.axis_index("slab") * count_a
    first_l = lax.axis_index("chan") * count_l
    inv_mult = 1.0 / multiplicity(
        count_l,
        count_a,
        first_l,
        first_a,
        count_l * lax.axis_size("chan"),
        count_a * lax.axis_size("slab"),
    )

    def local_apply(field):
        gradients = [
            forward(matrix, field, conjugate_update_vector) for conjugate_update_vector in range(3)
        ]
        summed = coolant_throughput * integration_factor * field
        summed = summed + backward(matrix, weighted_kappa * gradients[0], 0)
        summed = summed + backward(matrix, weighted_kappa * gradients[1], 1)
        summed = summed + backward(matrix, weighted_kappa * gradients[2], 2)
        mixed = backward(matrix, weighted_kappa * gradients[1], 0) + backward(
            matrix, weighted_kappa * gradients[0], 1
        )
        return summed + cross_el * mixed

    source_vector = gather_nodes(
        integration_factor * (coolant_throughput * previous_panel_warmth + pointwise_energy_source)
    )
    solved_panel_warmth = jnp.zeros_like(source_vector)
    residual = source_vector

    def squared_norm(vector_field):
        return lax.psum(jnp.sum(vector_field * vector_field * inv_mult), ("slab", "chan"))

    conjugate_update_vector = residual
    norm_now = squared_norm(residual)
    for number in range(ITERS):
        applied = gather_nodes(local_apply(conjugate_update_vector))
        conjugate_alpha_factor = norm_now / lax.psum(
            jnp.sum(conjugate_update_vector * applied * inv_mult), ("slab", "chan")
        )
        solved_panel_warmth = solved_panel_warmth + conjugate_alpha_factor * conjugate_update_vector
        residual = residual - conjugate_alpha_factor * applied
        norm_next = squared_norm(residual)
        conjugate_update_vector = residual + norm_next / norm_now * conjugate_update_vector
        norm_now = norm_next
    return (stepped_stream_speed, solved_panel_warmth)


def solution(mesh):
    in_specs = (
        P(None, None, None, None, ("slab", "chan")),
        P(("slab", "chan")),
        P(None, None, None, "chan", "slab"),
        P(None, None, None, "chan", "slab"),
        P("chan", "slab"),
        P("chan", "slab"),
    )
    out_specs = (P(None, None, None, None, ("slab", "chan")), P(None, None, None, "chan", "slab"))
    return jax.shard_map(
        on_device, mesh=mesh, in_specs=in_specs, out_specs=out_specs, check_vma=False
    )
```

profile of v0, /device:TPU:0, one launch (start us, length us, event | category | flops | bytes accessed | tf_op | source)
XLA Modules:
  0.0 1214.1 jit_solution(5461237540410165902)
XLA Ops:
  2.2 3.5 fusion.109
  6.1 3.9 collective-permute-start
  15.7 3.6 fusion.17
  21.1 4.6 fusion.5
  25.7 5.1 fusion.8
  32.6 21.1 %fusion.151 = (f32[3,8,8,8,512]{4,1,3,2,0:T(8,128)S(1)}, bf16[3,8,8,8,512]{4,1,3,2,0:T(8,128)(2,1)}) fusion(f32[8,3,8,8,512]{4,0,3,2,1:T(8,128)} %copy-done.8, f32[8,8,8,512]{3,0,2,1:T(8,128)} %get-tuple-element.597, f32[8,3,8,8,512]{4,0,3,2,1:T(8,128)} %copy-done.9, f32[8,8,8,512]{3,0,2,1:T(8,128)} %get-tuple-element.598, ...), kind=kOutput, calls=%fused_computation.324 | convolution fusion | flops 86507520 | bytes 25166080 | tf_op jit(solution)/shard_map/ir,crste->ciste/dot_general | solution.py:98
  54.9 3.0 scatter_fusion
  58.7 2.6 collective-permute-start.6
  61.4 5.6 collective-permute-start.5
  69.9 5.0 scatter.94
  77.9 23.3 %scatter.95 = f32[8,8,8,2,256]{4,0,3,2,1:T(8,128)S(1)} dynamic-update-slice(f32[8,8,8,2,256]{4,0,3,2,1:T(8,128)S(1)} %scatter.94, f32[1,8,8,2,255]{4,0,3,2,1:T(1,128)S(1)} %copy.422, s32[]{:T(128)S(1)} %bitcast.288, s32[]{:T(128)} %constant.1168.clone.1, s32[]{:T(128)} %constant.1168.clone.1, s32[]{:T(128)} %constant.1168.clone.1, s32[]{:T(128)} %bitcast.15) | dynamic-update-slice | bytes 261124 | tf_op jit(solution)/shard_map/scatter | solution.py:167
  101.5 2.2 scatter-add.80
  104.1 10.8 scatter-add.81
  120.9 2.6 fusion.105
  124.2 7.5 scatter_custom_fusion.1
  144.2 3.1 fusion.36
  152.9 7.0 scatter.104
  159.8 3.0 broadcast_select_fusion.4
  162.8 24.0 %scatter.105 = f32[8,8,8,2,256]{4,0,2,3,1:T(8,128)} dynamic-update-slice(f32[8,8,8,2,256]{4,0,2,3,1:T(8,128)} %scatter.104, f32[1,8,8,2,255]{4,0,2,3,1:T(1,128)S(1)} %broadcast_select_fusion.4, s32[]{:T(128)S(1)} %bitcast.291, s32[]{:T(128)} %constant.1168.clone.1, s32[]{:T(128)} %constant.1168.clone.1, s32[]{:T(128)} %constant.1168.clone.1, s32[]{:T(128)} %bitcast.15) | dynamic-update-slice | bytes 261124 | tf_op jit(solution)/shard_map/scatter | solution.py:167
  190.2 3.6 scatter-add.86
  195.3 12.3 %scatter-add.89 = f32[8,8,8,2,256]{4,0,2,3,1:T(8,128)} dynamic-update-slice(f32[8,8,8,2,256]{4,0,2,3,1:T(8,128)} %scatter-add.86, f32[1,8,8,2,1]{4,0,2,3,1:T(1,128)S(1)} %slice_add_fusion.28, s32[]{:T(128)} %constant.1167.clone.1, s32[]{:T(128)} %constant.1168.clone.1, s32[]{:T(128)} %constant.1168.clone.1, s32[]{:T(128)} %constant.1168.clone.1, s32[]{:T(128)} %constant.1172.clone.1) | dynamic-update-slice | bytes 1028 | tf_op jit(solution)/shard_map/scatter-add | solution.py:168
  209.7 3.8 collective-permute-start.9
  219.8 73.0 %all-reduce = (f32[]{:T(128)}, f32[]{:T(128)}) all-reduce(f32[]{:T(128)} %get-tuple-element.587, f32[]{:T(128)} %get-tuple-element.586), channel_id=1, replica_groups=mesh['slab'=16,'chan'=8] {'slab','chan'}, use_global_device_ids=true, to_apply=%region_3.4 | all-reduce | flops 2 | bytes 16 | tf_op jit(solution)/shard_map/psum | solution.py:253
  295.0 62.6 %psum.72 = f32[]{:T(128)} all-reduce(f32[]{:T(128)} %multiply_reduce_fusion.7), channel_id=1, replica_groups=mesh['slab'=16,'chan'=8] {'slab','chan'}, use_global_device_ids=true, to_apply=%region_13.14 | all-reduce | flops 1 | bytes 8 | tf_op jit(solution)/shard_map/psum | solution.py:253
  371.6 2.6 fusion.34
  379.6 3.9 collective-permute-start.11
  383.4 7.0 scatter.110
  390.4 3.6 broadcast_select_fusion.3
  394.0 24.0 %scatter.111 = f32[8,8,8,2,256]{4,0,2,3,1:T(8,128)} dynamic-update-slice(f32[8,8,8,2,256]{4,0,2,3,1:T(8,128)} %scatter.110, f32[1,8,8,2,255]{4,0,2,3,1:T(1,128)S(1)} %broadcast_select_fusion.3, s32[]{:T(128)S(1)} %bitcast.294, s32[]{:T(128)} %constant.1168.clone.1, s32[]{:T(128)} %constant.1168.clone.1, s32[]{:T(128)} %constant.1168.clone.1, s32[]{:T(128)} %bitcast.15) | dynamic-update-slice | bytes 261124 | tf_op jit(solution)/shard_map/scatter | solution.py:167
  422.0 3.7 scatter-add.94
  427.1 12.3 %scatter-add.95 = f32[8,8,8,2,256]{4,0,2,3,1:T(8,128)} dynamic-update-slice(f32[8,8,8,2,256]{4,0,2,3,1:T(8,128)} %scatter-add.94, f32[1,8,8,2,1]{4,0,2,3,1:T(1,128)S(1)} %slice_add_fusion.23, s32[]{:T(128)} %constant.1167.clone.1, s32[]{:T(128)} %constant.1168.clone.1, s32[]{:T(128)} %constant.1168.clone.1, s32[]{:T(128)} %constant.1168.clone.1, s32[]{:T(128)} %constant.1172.clone.1) | dynamic-update-slice | bytes 1028 | tf_op jit(solution)/shard_map/scatter-add | solution.py:168
  450.2 69.4 %psum.73 = f32[]{:T(128)} all-reduce(f32[]{:T(128)} %multiply_reduce_fusion.6), channel_id=1, replica_groups=mesh['slab'=16,'chan'=8] {'slab','chan'}, use_global_device_ids=true, to_apply=%region_15.16 | all-reduce | flops 1 | bytes 8 | tf_op jit(solution)/shard_map/psum | solution.py:259
  520.9 3.4 multiply_reduce_fusion.5
  524.3 64.0 %psum.74 = f32[]{:T(128)} all-reduce(f32[]{:T(128)} %get-tuple-element.594), channel_id=1, replica_groups=mesh['slab'=16,'chan'=8] {'slab','chan'}, use_global_device_ids=true, to_apply=%region_17.18 | all-reduce | flops 1 | bytes 8 | tf_op jit(solution)/shard_map/psum | solution.py:253
  602.2 2.6 fusion.30
  610.2 2.2 collective-permute-start.15
  612.4 7.0 scatter.116
  619.4 3.6 broadcast_select_fusion.2
  623.0 24.0 %scatter.119 = f32[8,8,8,2,256]{4,0,2,3,1:T(8,128)} dynamic-update-slice(f32[8,8,8,2,256]{4,0,2,3,1:T(8,128)} %scatter.116, f32[1,8,8,2,255]{4,0,2,3,1:T(1,128)S(1)} %broadcast_select_fusion.2, s32[]{:T(128)S(1)} %bitcast.297, s32[]{:T(128)} %constant.1168.clone.1, s32[]{:T(128)} %constant.1168.clone.1, s32[]{:T(128)} %constant.1168.clone.1, s32[]{:T(128)} %bitcast.15) | dynamic-update-slice | bytes 261124 | tf_op jit(solution)/shard_map/scatter | solution.py:167
  651.0 3.7 scatter-add.100
  656.1 12.3 %scatter-add.101 = f32[8,8,8,2,256]{4,0,2,3,1:T(8,128)} dynamic-update-slice(f32[8,8,8,2,256]{4,0,2,3,1:T(8,128)} %scatter-add.100, f32[1,8,8,2,1]{4,0,2,3,1:T(1,128)S(1)} %slice_add_fusion.18, s32[]{:T(128)} %constant.1167.clone.1, s32[]{:T(128)} %constant.1168.clone.1, s32[]{:T(128)} %constant.1168.clone.1, s32[]{:T(128)} %constant.1168.clone.1, s32[]{:T(128)} %constant.1172.clone.1) | dynamic-update-slice | bytes 1028 | tf_op jit(solution)/shard_map/scatter-add | solution.py:168
  675.6 2.8 collective-permute-done.18
  680.4 70.2 %psum.75 = f32[]{:T(128)} all-reduce(f32[]{:T(128)} %multiply_reduce_fusion.4), channel_id=1, replica_groups=mesh['slab'=16,'chan'=8] {'slab','chan'}, use_global_device_ids=true, to_apply=%region_19.20 | all-reduce | flops 1 | bytes 8 | tf_op jit(solution)/shard_map/psum | solution.py:259
  751.8 3.4 multiply_reduce_fusion.3
  755.3 62.5 %psum.76 = f32[]{:T(128)} all-reduce(f32[]{:T(128)} %get-tuple-element.592), channel_id=1, replica_groups=mesh['slab'=16,'chan'=8] {'slab','chan'}, use_global_device_ids=true, to_apply=%region_21.22 | all-reduce | flops 1 | bytes 8 | tf_op jit(solution)/shard_map/psum | solution.py:253
  832.2 2.6 fusion.26
  840.2 4.2 collective-permute-start.19
  844.3 7.0 scatter.124
  851.3 3.6 broadcast_select_fusion.1
  854.9 24.0 %scatter.125 = f32[8,8,8,2,256]{4,0,2,3,1:T(8,128)} dynamic-update-slice(f32[8,8,8,2,256]{4,0,2,3,1:T(8,128)} %scatter.124, f32[1,8,8,2,255]{4,0,2,3,1:T(1,128)S(1)} %broadcast_select_fusion.1, s32[]{:T(128)S(1)} %bitcast.300, s32[]{:T(128)} %constant.1168.clone.1, s32[]{:T(128)} %constant.1168.clone.1, s32[]{:T(128)} %constant.1168.clone.1, s32[]{:T(128)} %bitcast.15) | dynamic-update-slice | bytes 261124 | tf_op jit(solution)/shard_map/scatter | solution.py:167
  882.9 3.7 scatter-add.106
  888.0 12.3 %scatter-add.109 = f32[8,8,8,2,256]{4,0,2,3,1:T(8,128)} dynamic-update-slice(f32[8,8,8,2,256]{4,0,2,3,1:T(8,128)} %scatter-add.106, f32[1,8,8,2,1]{4,0,2,3,1:T(1,128)S(1)} %slice_add_fusion.13, s32[]{:T(128)} %constant.1167.clone.1, s32[]{:T(128)} %constant.1168.clone.1, s32[]{:T(128)} %constant.1168.clone.1, s32[]{:T(128)} %constant.1168.clone.1, s32[]{:T(128)} %constant.1172.clone.1) | dynamic-update-slice | bytes 1028 | tf_op jit(solution)/shard_map/scatter-add | solution.py:168
  911.0 69.1 %psum.77 = f32[]{:T(128)} all-reduce(f32[]{:T(128)} %multiply_reduce_fusion.2), channel_id=1, replica_groups=mesh['slab'=16,'chan'=8] {'slab','chan'}, use_global_device_ids=true, to_apply=%region_23.24 | all-reduce | flops 1 | bytes 8 | tf_op jit(solution)/shard_map/psum | solution.py:259
  981.4 2.4 multiply_reduce_fusion.1
  983.8 63.9 %psum.78 = f32[]{:T(128)} all-reduce(f32[]{:T(128)} %multiply_reduce_fusion.1), channel_id=1, replica_groups=mesh['slab'=16,'chan'=8] {'slab','chan'}, use_global_device_ids=true, to_apply=%region_25.26 | all-reduce | flops 1 | bytes 8 | tf_op jit(solution)/shard_map/psum | solution.py:253
  1062.5 2.4 fusion.22
  1069.8 7.0 scatter.156
  1076.8 3.0 broadcast_select_fusion
  1079.8 24.0 %scatter.157 = f32[8,8,8,2,256]{4,0,2,3,1:T(8,128)} dynamic-update-slice(f32[8,8,8,2,256]{4,0,2,3,1:T(8,128)} %scatter.156, f32[1,8,8,2,255]{4,0,2,3,1:T(1,128)S(1)} %broadcast_select_fusion, s32[]{:T(128)S(1)} %bitcast.303, s32[]{:T(128)} %constant.1168.clone.1, s32[]{:T(128)} %constant.1168.clone.1, s32[]{:T(128)} %constant.1168.clone.1, s32[]{:T(128)} %bitcast.15) | dynamic-update-slice | bytes 261124 | tf_op jit(solution)/shard_map/scatter | solution.py:167
  1106.5 3.7 scatter-add.114
  1111.6 12.3 %scatter-add.115 = f32[8,8,8,2,256]{4,0,2,3,1:T(8,128)} dynamic-update-slice(f32[8,8,8,2,256]{4,0,2,3,1:T(8,128)} %scatter-add.114, f32[1,8,8,2,1]{4,0,2,3,1:T(1,128)S(1)} %slice_add_fusion.8, s32[]{:T(128)} %constant.1167.clone.1, s32[]{:T(128)} %constant.1168.clone.1, s32[]{:T(128)} %constant.1168.clone.1, s32[]{:T(128)} %constant.1168.clone.1, s32[]{:T(128)} %constant.1172.clone.1) | dynamic-update-slice | bytes 1028 | tf_op jit(solution)/shard_map/scatter-add | solution.py:168
  1131.3 2.8 collective-permute-done.26
  1134.0 2.2 multiply_reduce_fusion
  1137.9 71.0 %psum.79 = f32[]{:T(128)} all-reduce(f32[]{:T(128)} %multiply_reduce_fusion), channel_id=1, replica_groups=mesh['slab'=16,'chan'=8] {'slab','chan'}, use_global_device_ids=true, to_apply=%region_27.28 | all-reduce | flops 1 | bytes 8 | tf_op jit(solution)/shard_map/psum | solution.py:259
  (299 shorter events, 194.7 us)
Async XLA Ops:
  0.6 11.1 copy-start.6
  5.7 6.9 copy-start.17
  6.1 95.1 %collective-permute-start = (f32[1,8,8,2]{2,1,3,0:T(8,128)S(1)}, f32[1,8,8,2]{2,1,3,0:T(8,128)S(1)}, u32[]{:S(2)}, u32[]{:S(2)}) collective-permute-start(f32[1,8,8,2]{2,1,3,0:T(8,128)S(1)} %bitcast.308), channel_id=1, source_target_pairs={{0,8},{8,16},{16,24},{24,32},{32,40},{40,48},{48,56},{56,64},{64,7... | collective-permute-start | bytes 1544 | tf_op jit(solution)/shard_map/ppermute | solution.py:34
  10.2 93.5 %collective-permute-start.1 = (f32[1,8,8,2]{2,1,3,0:T(8,128)S(1)}, f32[1,8,8,2]{2,1,3,0:T(8,128)S(1)}, u32[]{:S(2)}, u32[]{:S(2)}) collective-permute-start(f32[1,8,8,2]{2,1,3,0:T(8,128)S(1)} %bitcast.306), channel_id=1, source_target_pairs={{8,0},{16,8},{24,16},{32,24},{40,32},{48,40},{56,48},{64,56},{72,6... | collective-permute-start | bytes 1544 | tf_op jit(solution)/shard_map/ppermute | solution.py:35
  14.1 7.0 copy-start.8
  15.7 10.0 copy-start.9
  25.7 5.1 copy-start.26
  25.7 6.8 copy-start.29
  54.8 20.1 %copy-start.31 = (s32[5]{0:T(128)S(1)}, s32[5]{0:T(128)}, u32[]{:S(2)}) copy-start(s32[5]{0:T(128)} %constant.1170.clone.1) | copy-start | bytes 64
  54.9 20.7 %copy-start.27 = (s32[2,256]{1,0:T(2,128)S(1)}, s32[2,256]{1,0:T(2,128)}, u32[]{:S(2)}) copy-start(s32[2,256]{1,0:T(2,128)} %param.109) | copy-start | bytes 6148
  54.9 20.7 %copy-start.28 = (s32[2,256]{1,0:T(2,128)S(1)}, s32[2,256]{1,0:T(2,128)}, u32[]{:S(2)}) copy-start(s32[2,256]{1,0:T(2,128)} %param.110) | copy-start | bytes 6148
  54.9 22.2 %copy-start.30 = (s32[5]{0:T(128)S(1)}, s32[5]{0:T(128)}, u32[]{:S(2)}) copy-start(s32[5]{0:T(128)} %constant.1173.clone.1) | copy-start | bytes 64
  58.7 64.8 %collective-permute-start.6 = (bf16[514,128]{0,1:T(8,128)(2,1)}, bf16[514,128]{0,1:T(8,128)(2,1)S(1)}, u32[]{:S(2)}, u32[]{:S(2)}) collective-permute-start(bf16[514,128]{0,1:T(8,128)(2,1)} %get-tuple-element.641), channel_id=1, source_target_pairs={{120,0},{121,1},{122,2},{123,3},{124,4},{125,5},{126,6},{127,7},{0... | collective-permute-start | bytes 394760 | tf_op jit(solution)/shard_map/ppermute | solution.py:24
  61.4 62.2 %collective-permute-start.5 = (bf16[514,128]{0,1:T(8,128)(2,1)}, bf16[514,128]{0,1:T(8,128)(2,1)S(1)}, u32[]{:S(2)}, u32[]{:S(2)}) collective-permute-start(bf16[514,128]{0,1:T(8,128)(2,1)} %get-tuple-element.642), channel_id=1, source_target_pairs={{1,0},{2,1},{3,2},{4,3},{5,4},{6,5},{7,6},{8,7},{9,8},{10,9},{11,1... | collective-permute-start | bytes 394760 | tf_op jit(solution)/shard_map/ppermute | solution.py:24
  67.0 56.5 %collective-permute-start.4 = (bf16[514,128]{0,1:T(8,128)(2,1)}, bf16[514,128]{0,1:T(8,128)(2,1)S(1)}, u32[]{:S(2)}, u32[]{:S(2)}) collective-permute-start(bf16[514,128]{0,1:T(8,128)(2,1)} %get-tuple-element.640), channel_id=1, source_target_pairs={{127,0},{0,1},{1,2},{2,3},{3,4},{4,5},{5,6},{6,7},{7,8},{8,9},{9,1... | collective-permute-start | bytes 394760 | tf_op jit(solution)/shard_map/ppermute | solution.py:24
  75.6 68.6 %copy-start.21 = (f32[2,256]{1,0:T(2,128)}, f32[2,256]{1,0:T(2,128)S(1)}, u32[]{:S(2)}) copy-start(f32[2,256]{1,0:T(2,128)S(1)} %get-tuple-element.645) | copy-start | bytes 6148
  115.1 3.9 collective-permute-start.2
  116.4 3.1 collective-permute-start.3
  123.5 0.7 copy-start.19
  134.8 3.2 copy-start.18
  139.8 3.3 copy-start.20
  151.0 37.2 %collective-permute-start.7 = (f32[1,8,8,2]{2,1,3,0:T(8,128)}, f32[1,8,8,2]{2,1,3,0:T(8,128)}, u32[]{:S(2)}, u32[]{:S(2)}) collective-permute-start(f32[1,8,8,2]{2,1,3,0:T(8,128)} %bitcast.312), channel_id=1, source_target_pairs={{0,8},{8,16},{16,24},{24,32},{32,40},{40,48},{48,56},{56,64},{64,7... | collective-permute-start | bytes 1544 | tf_op jit(solution)/shard_map/ppermute | solution.py:34
  186.9 6.9 collective-permute-start.8
  209.7 7.2 collective-permute-start.9
  215.6 3.1 collective-permute-start.10
  218.8 138.8 %copy-start.7 = (f32[8,8,8,2,256]{4,0,2,3,1:T(8,128)}, f32[8,8,8,2,256]{4,0,2,3,1:T(8,128)S(1)}, u32[]{:S(2)}) copy-start(f32[8,8,8,2,256]{4,0,2,3,1:T(8,128)S(1)} %fusion.123) | copy-start | bytes 3145732
  371.5 2.6 copy-start.22
  375.8 1.4 copy-start.13
  379.6 40.4 %collective-permute-start.11 = (f32[1,8,8,2]{2,1,3,0:T(8,128)}, f32[1,8,8,2]{2,1,3,0:T(8,128)}, u32[]{:S(2)}, u32[]{:S(2)}) collective-permute-start(f32[1,8,8,2]{2,1,3,0:T(8,128)} %bitcast.313), channel_id=1, source_target_pairs={{0,8},{8,16},{16,24},{24,32},{32,40},{40,48},{48,56},{56,64},{64,7... | collective-permute-start | bytes 1544 | tf_op jit(solution)/shard_map/ppermute | solution.py:34
  418.7 6.9 collective-permute-start.12
  441.5 4.8 collective-permute-start.13
  445.0 3.3 collective-permute-start.14
  448.3 1.0 copy-start.11
  590.9 11.4 copy-start
  602.2 2.6 copy-start.23
  606.4 1.4 copy-start.14
  610.2 38.8 %collective-permute-start.15 = (f32[1,8,8,2]{2,1,3,0:T(8,128)}, f32[1,8,8,2]{2,1,3,0:T(8,128)}, u32[]{:S(2)}, u32[]{:S(2)}) collective-permute-start(f32[1,8,8,2]{2,1,3,0:T(8,128)} %bitcast.314), channel_id=1, source_target_pairs={{0,8},{8,16},{16,24},{24,32},{32,40},{40,48},{48,56},{56,64},{64,7... | collective-permute-start | bytes 1544 | tf_op jit(solution)/shard_map/ppermute | solution.py:34
  647.7 7.0 collective-permute-start.16
  668.4 11.0 copy-start.1
  670.6 5.0 collective-permute-start.17
  674.3 4.1 collective-permute-start.18
  678.4 1.0 copy-start.12
  820.8 11.4 copy-start.3
  832.2 2.6 copy-start.24
  836.4 1.4 copy-start.15
  840.2 40.7 %collective-permute-start.19 = (f32[1,8,8,2]{2,1,3,0:T(8,128)}, f32[1,8,8,2]{2,1,3,0:T(8,128)}, u32[]{:S(2)}, u32[]{:S(2)}) collective-permute-start(f32[1,8,8,2]{2,1,3,0:T(8,128)} %bitcast.315), channel_id=1, source_target_pairs={{0,8},{8,16},{16,24},{24,32},{32,40},{40,48},{48,56},{56,64},{64,7... | collective-permute-start | bytes 1544 | tf_op jit(solution)/shard_map/ppermute | solution.py:34
  879.6 7.0 collective-permute-start.20
  900.2 9.9 copy-start.4
  902.5 4.8 collective-permute-start.21
  905.9 3.1 collective-permute-start.22
  909.1 1.0 copy-start.10
  1051.1 11.4 copy-start.5
  1062.5 2.4 copy-start.25
  1068.2 37.0 %collective-permute-start.23 = (f32[1,8,8,2]{2,1,3,0:T(8,128)S(1)}, f32[1,8,8,2]{2,1,3,0:T(8,128)S(1)}, u32[]{:S(2)}, u32[]{:S(2)}) collective-permute-start(f32[1,8,8,2]{2,1,3,0:T(8,128)S(1)} %bitcast.310), channel_id=1, source_target_pairs={{0,8},{8,16},{16,24},{24,32},{32,40},{40,48},{48,56},{56,64},{64,7... | collective-permute-start | bytes 1544 | tf_op jit(solution)/shard_map/ppermute | solution.py:34
  1103.9 6.3 collective-permute-start.24
  1123.9 12.3 %copy-start.16 = (bf16[3,8,8,8,512]{4,1,3,2,0:T(8,128)(2,1)S(1)}, bf16[3,8,8,8,512]{4,1,3,2,0:T(8,128)(2,1)}, u32[]{:S(2)}) copy-start(bf16[3,8,8,8,512]{4,1,3,2,0:T(8,128)(2,1)} %get-tuple-element.651) | copy-start | bytes 4718596
  1126.1 84.0 %copy-start.2 = (f32[8,8,8,2,256]{4,0,2,3,1:T(8,128)S(1)}, f32[8,8,8,2,256]{4,0,2,3,1:T(8,128)}, u32[]{:S(2)}) copy-start(f32[8,8,8,2,256]{4,0,2,3,1:T(8,128)} %copy-done) | copy-start | bytes 3145732
  1126.1 5.1 collective-permute-start.25
  1129.9 4.1 collective-permute-start.26
where the time goes:
time: 1220 us; the launch traced here: 1210 us
  blocking collectives  606 us (50%)
  local copies, waits for them, and re-layouts  324 us (27%)
  matrix products  106 us (9%)
  other arithmetic  100 us (8%)
  starting transfers between devices  52.3 us (4%)
  between operations  13.9 us (1%)
    psum x5, blocking collectives, squared_norm(): lax.psum(jnp.sum(vector_field * vector_field * inv_mult), ('slab', 'chan'))  326 us
    psum x4, blocking collectives, on_device(): lax.psum(jnp.sum(conjugate_update_vector * applied * inv_mult), ('slab',...  280 us
    scatter x12, local copies, waits for them, and re-layouts, gather_nodes(): field = field.at[7, :, :, :, :-1].set(shared).at[0, :, :, :, 1:].set(shared)  183 us
    scatter-add x13, local copies, waits for them, and re-layouts, gather_nodes(): field.at[0, :, :, :, 0].add(with_rims[0]).at[7, :, :, :, -1]  92.8 us
    dot_general x25, matrix products, backward(): jnp.einsum(backward_forms[conjugate_update_vector], matrix, field, precis...  45.1 us
    ppermute x12, starting transfers between devices, with_halo(): before = lax.ppermute(last, axis, up)  28.4 us
  transfers between devices with their start and end apart: 27, of which 6 were waited for; matrix products, arithmetic and copies ran while one was open for 26% of the time, Pallas kernels for 0%

commit v1 on v0

v1 whole, which is shorter than its diff:
```python
import functools

import jax
import jax.numpy as jnp
import numpy as np
from jax import lax
from jax.experimental import pallas as pl
from jax.experimental.pallas import tpu as pltpu
from jax.sharding import PartitionSpec as P

F32 = jnp.float32
BF16 = jnp.bfloat16
MESH = pl.DeviceIdType.MESH
ITERS = 5
SCALE = 64.0
NT = (((1,), (1,)), ((), ()))
NN = (((1,), (0,)), ((), ()))


def gll():
    points = np.array(
        [
            -1.0,
            -0.8717401485096066,
            -0.5917001814331423,
            -0.2092992179024789,
            0.2092992179024789,
            0.5917001814331423,
            0.8717401485096066,
            1.0,
        ]
    )
    weights = np.array(
        [
            1.0 / 28.0,
            0.2107042271435061,
            0.3411226924835044,
            0.4124587946587038,
            0.4124587946587038,
            0.3411226924835044,
            0.2107042271435061,
            1.0 / 28.0,
        ]
    )
    low = np.ones(8)
    high = points.copy()
    for degree in range(1, 7):
        low, high = high, ((2 * degree + 1) * points * high - degree * low) / (degree + 1)
    gaps = points[:, None] - points[None, :] + np.eye(8)
    deriv = high[:, None] / (high[None, :] * gaps)
    deriv = deriv * (1.0 - np.eye(8))
    deriv[0, 0] = -14.0
    deriv[7, 7] = 14.0
    return deriv, weights


def two(matrix):
    high = np.asarray(matrix, np.float32).astype(BF16).astype(np.float64)
    return high, matrix - high


def operators():
    deriv, weights = gll()
    second = deriv @ deriv
    eye = np.eye
    kron = np.kron
    along_s = kron(eye(4), kron(deriv, eye(8)))
    along_t = kron(eye(32), deriv)
    along_r = kron(deriv, eye(32))
    ds_hi, ds_lo = two(along_s)
    dt_hi, dt_lo = two(along_t)
    dr_hi, dr_lo = two(along_r)
    fwd_st = np.block([[ds_hi, ds_lo, ds_hi], [dt_hi, dt_lo, dt_hi]])
    fwd_r = np.block([[dr_hi, dr_lo, dr_hi]])
    bwd_st = np.block([[ds_hi.T, dt_hi.T, ds_lo.T, dt_lo.T, ds_hi.T, dt_hi.T]])
    bwd_r = np.block([[dr_hi.T, dr_lo.T, dr_hi.T]])
    flu_st = np.block([[ds_hi, ds_lo], [dt_hi, dt_lo]])
    flu_r = np.block([[dr_hi, dr_lo]])
    lap_st = kron(eye(4), kron(second, eye(8))) + kron(eye(32), second)
    lap_r = kron(second, eye(32))
    volume = (weights[:, None, None] * weights[None, :, None] * weights[None, None, :]).reshape(512, 1)
    cast = lambda m: jnp.asarray(np.asarray(m, np.float32).astype(BF16))
    return {
        "fwd_st": cast(fwd_st),
        "fwd_r": cast(fwd_r),
        "bwd_st": cast(bwd_st),
        "bwd_r": cast(bwd_r),
        "flu_st": cast(flu_st),
        "flu_r": cast(flu_r),
        "lap_st": cast(lap_st),
        "lap_r": cast(lap_r),
        "volume": jnp.asarray(np.broadcast_to(volume, (512, 128)), F32),
    }


def dot(a, b, dims=NN):
    return lax.dot_general(a, b, dims, preferred_element_type=F32)


def iota(shape, dim):
    return lax.broadcasted_iota(jnp.int32, shape, dim)


def fluid_kernel(
    u_ref, index_ref, flu_st, flu_r, lap_st, lap_r, out_ref, pack_ref, grad, lap, cond
):
    step = pl.program_id(0)
    lanes = u_ref.shape[2]

    def component(c, square):
        field = u_ref[pl.ds(c * 64, 64)].astype(F32)
        flat = field.reshape(512, lanes)
        low = flat.astype(BF16)
        for h in range(2):
            rows = pl.ds(256 * h, 256)
            part = low[256 * h : 256 * h + 256]
            both = dot(flu_st[...], jnp.concatenate([part, part], 0))
            grad[1, rows] = both[:256]
            grad[2, rows] = both[256:]
            lap[rows] = dot(lap_st[...], part)
        by_r = flat.reshape(8, 64, lanes)
        for q in range(2):
            part = by_r[:, 32 * q : 32 * q + 32].reshape(256, lanes).astype(BF16)
            one = dot(flu_r[...], jnp.concatenate([part, part], 0)).reshape(8, 32, lanes)
            more = dot(lap_r[...], part).reshape(8, 32, lanes)
            for r in range(8):
                rows = pl.ds(64 * r + 32 * q, 32)
                grad[0, rows] = one[r]
                lap[rows] = lap[rows] + more[r]
        u0 = u_ref[0:64].astype(F32).reshape(512, lanes)
        u1 = u_ref[64:128].astype(F32).reshape(512, lanes)
        u2 = u_ref[128:192].astype(F32).reshape(512, lanes)
        convect = u0 * grad[0] + u1 * grad[1] + u2 * grad[2]
        new = (flat + 0.01 * (0.02 * lap[...] - convect)).astype(BF16)
        new32 = new.astype(F32)
        out_ref[pl.ds(c * 64, 64)] = new32.reshape(64, 8, lanes).astype(BF16)
        return square + new32 * new32

    square = jnp.zeros((512, lanes), F32)
    for c in range(3):
        square = component(c, square)
    cond[0:512, pl.ds(pl.multiple_of(step * lanes, lanes), lanes)] = (1.0 + 0.5 * square).astype(BF16)

    @pl.when(step == pl.num_programs(0) - 1)
    def _():
        total = lax.axis_size("slab") * lax.axis_size("chan")
        chans = lax.axis_size("chan")
        me = lax.axis_index("slab") * chans + lax.axis_index("chan")
        target = index_ref[...]
        device = target >> 9
        slot = target & 511
        distance = (device - me) & (total - 1)
        group = jnp.where(
            distance == 1,
            1,
            jnp.where(distance == total - 1, 2, jnp.where(distance == chans, 3, 0)),
        )
        member = iota((8, 512), 0) == group
        before = (iota((512, 512), 0) < iota((512, 512), 1)).astype(F32).astype(BF16)
        rank = dot(member.astype(F32).astype(BF16), before)
        start = jnp.where(
            iota((8, 512), 0) == 0, 0, 128 + 128 * iota((8, 512), 0)
        ).astype(F32)
        position = jnp.sum(jnp.where(member, rank + start, 0.0), axis=0, keepdims=True).astype(jnp.int32)
        code = jnp.where(
            iota((16, 512), 0) == 0,
            (slot >> 5) + 1,
            jnp.where(iota((16, 512), 0) == 1, slot & 31, 0),
        )
        cond[512:528] = code.astype(F32).astype(BF16)
        for k in range(5):
            chosen = (iota((128, 512), 0) + 128 * k == position).astype(F32).astype(BF16)
            pack_ref[k] = dot(cond[...], chosen, NT).astype(BF16)


def fluid(u, index, ops):
    blocks = 2
    lanes = 512 // blocks
    fixed = lambda shape: pl.BlockSpec(shape, lambda i: (0,) * len(shape))
    return pl.pallas_call(
        fluid_kernel,
        grid=(blocks,),
        in_specs=[
            pl.BlockSpec((192, 8, lanes), lambda i: (0, 0, i)),
            fixed((1, 512)),
            fixed((512, 512)),
            fixed((256, 512)),
            fixed((256, 256)),
            fixed((256, 256)),
        ],
        out_specs=[
            pl.BlockSpec((192, 8, lanes), lambda i: (0, 0, i)),
            fixed((5, 528, 128)),
        ],
        out_shape=[
            jax.ShapeDtypeStruct((192, 8, 512), BF16),
            jax.ShapeDtypeStruct((5, 528, 128), BF16),
        ],
        scratch_shapes=[
            pltpu.VMEM((3, 512, lanes), F32),
            pltpu.VMEM((512, lanes), F32),
            pltpu.VMEM((528, 512), BF16),
        ],
        name="fluid",
    )(u, index, ops["flu_st"], ops["flu_r"], ops["lap_st"], ops["lap_r"])


def krylov_weights(m):
    n = ITERS
    zero = jnp.zeros_like(m[0])
    older, newer = [zero] * (2 * n), list(m)
    diag = [newer[1] / newer[0]]
    off = [zero]
    for k in range(1, n):
        fresh = [zero] * (2 * n)
        for l in range(k, 2 * n - k):
            fresh[l] = newer[l + 1] - diag[k - 1] * newer[l] - off[k - 1] * older[l]
        diag.append(fresh[k + 1] / fresh[k] - newer[k] / newer[k - 1])
        off.append(fresh[k] / newer[k - 1])
        older, newer = newer, fresh
    alpha = [1.0 / diag[0]]
    beta = []
    for k in range(1, n):
        beta.append(off[k] * alpha[k - 1] * alpha[k - 1])
        alpha.append(1.0 / (diag[k] - beta[k - 1] / alpha[k - 1]))
    one = jnp.ones_like(zero)
    res, way, sol = [one], [one], [zero] * n
    for k in range(n):
        for i in range(k + 1):
            sol[i] = sol[i] + alpha[k] * way[i]
        if k < n - 1:
            res = res + [zero]
            for i in range(k + 1):
                res[i + 1] = res[i + 1] - alpha[k] * way[i]
            way = [res[i] + (beta[k] * way[i] if i <= k else 0.0) for i in range(k + 2)]
    return sol


HALO = ((1, 0), (-1, 0), (0, 1), (0, -1), (1, 1), (1, -1), (-1, 1), (-1, -1))


def panel_kernel(
    n_slab,
    n_chan,
    pack_ref,
    prev_ref,
    source_ref,
    flag_ref,
    ply_ref,
    fwd_st,
    fwd_r,
    bwd_st,
    bwd_r,
    volume_ref,
    out_ref,
    basis,
    kap,
    inv_mult,
    grad,
    flux,
    acc,
    got_pack,
    edge_out,
    edge_in,
    side_out,
    side_in,
    chan_sum,
    slab_sum,
    pack_send,
    pack_recv,
    halo_send,
    halo_recv,
    chan_send,
    chan_recv,
    slab_send,
    slab_recv,
):
    slab = lax.axis_index("slab")
    chan = lax.axis_index("chan")
    device = slab * n_chan + chan
    devices = n_slab * n_chan

    def near(ds, dc):
        return (lax.rem(slab + ds + n_slab, n_slab), lax.rem(chan + dc + n_chan, n_chan))

    barrier = pltpu.get_barrier_semaphore()
    greet = [near(*d) for d in HALO]
    greet += [(slab, lax.rem(chan + j, n_chan)) for j in range(2, n_chan - 1)]
    greet += [(lax.rem(slab + j, n_slab), chan) for j in range(2, n_slab - 1)]
    for peer in greet:
        pl.semaphore_signal(barrier, inc=1, device_id=peer, device_id_type=MESH)

    for l in range(2):
        for h in range(2):
            lane = pl.ds(256 * l + 128 * h, 128)
            rows = pl.ds(2 * h + l, 512, stride=4)
            value = volume_ref[...] * (0.05 * prev_ref[rows, :] + source_ref[rows, :])
            basis[0, :, :, :, lane] = value.reshape(8, 8, 8, 128)
    node = iota((512, 128), 0)
    at_r = node >> 6
    at_s = (node >> 3) & 7
    for l in range(2):
        for h in range(2):
            lane = pl.ds(256 * l + 128 * h, 128)
            axial = slab * 256 + 128 * h + iota((512, 128), 1)
            m_r = jnp.where(((at_r == 0) & (axial > 0)) | ((at_r == 7) & (axial < n_slab * 256 - 1)), 0.5, 1.0)
            lateral = chan * 2 + l
            m_s = jnp.where(((at_s == 0) & (lateral > 0)) | ((at_s == 7) & (lateral < n_chan * 2 - 1)), 0.5, 1.0)
            inv_mult[:, lane] = m_r * m_s
    flag = jnp.concatenate([flag_ref[0:1], flag_ref[1:2]], 1)
    ply = jnp.concatenate([ply_ref[0:1], ply_ref[1:2]], 1).astype(F32)
    damping = jnp.where(flag == 1, 1.0 / (1.0 + 0.25 * ply), 1.0)
    cross = 0.4 * flag.astype(F32) * ply / (ply + 1.0)

    pl.semaphore_wait(barrier, len(greet))

    def device_at(step):
        number = lax.rem(device + step + devices, devices)
        return (number // n_chan, lax.rem(number, n_chan))

    moves = []
    for k, step in enumerate((1, -1, n_chan)):
        copy = pltpu.make_async_remote_copy(
            src_ref=pack_ref.at[2 + k],
            dst_ref=got_pack.at[k],
            send_sem=pack_send.at[k],
            recv_sem=pack_recv.at[k],
            device_id=device_at(step),
            device_id_type=MESH,
        )
        copy.start()
        moves.append(copy)

    lane8 = iota((8, 128), 1)
    has_left = slab > 0
    has_right = slab < n_slab - 1
    has_under = chan > 0
    has_over = chan < n_chan - 1

    def halo_copies(i):
        copies = []
        for d, (ds, dc) in enumerate(HALO):
            if ds == 0:
                k = 0 if dc == 1 else 1
                src, dst = side_out.at[i, k], side_in.at[i, k]
            else:
                src, dst = edge_out.at[i, 0 if ds == 1 else 1], edge_in.at[i, d]
            copies.append(
                pltpu.make_async_remote_copy(
                    src_ref=src,
                    dst_ref=dst,
                    send_sem=halo_send.at[i, d],
                    recv_sem=halo_recv.at[i, d],
                    device_id=near(ds, dc),
                    device_id_type=MESH,
                )
            )
        return copies

    def assemble_start(i):
        up = jnp.zeros((8, 128), F32)
        down = jnp.zeros((8, 128), F32)
        for l in range(2):
            for s in range(8):
                to = s + 8 * l
                here = lane8 == to
                last = basis[i, 7, s, :, 256 * l + 128 : 256 * l + 256]
                up = jnp.where(here, pltpu.roll(last, (to - 127) % 128, 1), up)
                first = basis[i, 0, s, :, 256 * l : 256 * l + 128]
                down = jnp.where(here, pltpu.roll(first, to, 1), down)
        edge_out[i, 0] = up
        edge_out[i, 1] = down
        copies = halo_copies(i)
        for d, (ds, dc) in enumerate(HALO):
            if ds != 0:
                copies[d].start()
        lane_a = iota((64, 256), 1)
        for l in range(2):
            lane = pl.ds(256 * l, 256)
            high = basis[i, 7, :, :, lane].reshape(64, 256)
            low = basis[i, 0, :, :, lane].reshape(64, 256)
            basis[i, 7, :, :, lane] = (
                high + jnp.where(lane_a == 255, 0.0, pltpu.roll(low, 255, 1))
            ).reshape(8, 8, 256)
            basis[i, 0, :, :, lane] = (
                low + jnp.where(lane_a == 0, 0.0, pltpu.roll(high, 1, 1))
            ).reshape(8, 8, 256)
        side_out[i, 0] = basis[i, :, 7, :, 256:512]
        side_out[i, 1] = basis[i, :, 0, :, 0:256]
        for d, (ds, dc) in enumerate(HALO):
            if ds == 0:
                copies[d].start()
        both = basis[i, :, 7, :, 0:256] + basis[i, :, 0, :, 256:512]
        basis[i, :, 7, :, 0:256] = both
        basis[i, :, 0, :, 256:512] = both

    def assemble_end(i):
        copies = halo_copies(i)
        for copy in copies:
            copy.wait()
        from_left = edge_in[i, 0]
        from_right = edge_in[i, 1]
        first = lane8 == 0
        last = lane8 == 127
        for l in range(2):
            for s in range(8):
                at = s + 8 * l
                lane0 = pl.ds(256 * l, 128)
                lane1 = pl.ds(256 * l + 128, 128)
                basis[i, 0, s, :, lane0] += jnp.where(
                    first & has_left, pltpu.roll(from_left, (128 - at) % 128, 1), 0.0
                )
                basis[i, 7, s, :, lane1] += jnp.where(
                    last & has_right, pltpu.roll(from_right, (127 - at) % 128, 1), 0.0
                )
        for k, (has, dc, at, s, l) in enumerate(
            ((has_under, 1, 15, 0, 0), (has_over, -1, 0, 7, 1))
        ):
            lane0 = pl.ds(256 * l, 128)
            lane1 = pl.ds(256 * l + 128, 128)
            face = side_in[i, k]
            basis[i, :, s, :, 256 * l : 256 * l + 256] += jnp.where(has, face, 0.0)
            left = edge_in[i, HALO.index((1, dc))]
            right = edge_in[i, HALO.index((-1, dc))]
            basis[i, 0, s, :, lane0] += jnp.where(
                first & has_left & has, pltpu.roll(left, (128 - at) % 128, 1), 0.0
            )
            basis[i, 7, s, :, lane1] += jnp.where(
                last & has_right & has, pltpu.roll(right, (127 - at) % 128, 1), 0.0
            )

    assemble_start(0)

    def place(slots, block):
        code = block[512:528].astype(F32)
        slot = ((code[0:1] - 1.0) * 32.0 + code[1:2]).astype(jnp.int32)
        chosen = (iota((512, 128), 0) == slot).astype(F32).astype(BF16)
        value = dot(block[0:512], chosen, NT)
        return value if slots is None else slots + value

    moved = place(place(None, pack_ref[0]), pack_ref[1])
    for k in range(3):
        moves[k].wait()
        moved = place(moved, got_pack[k])
    for h in range(4):
        lane = pl.ds(128 * h, 128)
        kap[:, lane] = (
            volume_ref[...] * (1.0 / SCALE) * moved[:, 128 * h : 128 * h + 128] * damping[:, 128 * h : 128 * h + 128]
        )

    assemble_end(0)

    def cut(x):
        high = x.astype(BF16)
        return high, (x - high.astype(F32)).astype(BF16)

    def gradient(i, lane):
        for h in range(2):
            field = basis[i, 4 * h : 4 * h + 4, :, :, lane].reshape(256, 256)
            high, low = cut(field)
            both = dot(fwd_st[...], jnp.concatenate([high, high, low], 0))
            grad[1, pl.ds(256 * h, 256)] = both[:256]
            grad[2, pl.ds(256 * h, 256)] = both[256:]
        for q in range(2):
            field = basis[i, :, 4 * q : 4 * q + 4, :, lane].reshape(256, 256)
            high, low = cut(field)
            one = dot(fwd_r[...], jnp.concatenate([high, high, low], 0)).reshape(8, 32, 256)
            for r in range(8):
                grad[0, pl.ds(64 * r + 32 * q, 32)] = one[r]

    def fold(x):
        total = jnp.sum(x.reshape(64, 8, 256), axis=0)
        return total[:, :128] + total[:, 128:]

    acc[...] = jnp.zeros_like(acc)

    def norm(i, block):
        lane = pl.ds(256 * block, 256)
        field = basis[i, :, :, :, lane].reshape(512, 256)
        acc[2 * i] += fold(field * field * inv_mult[:, lane])

    def volume2():
        v = volume_ref[...] * (0.05 / SCALE)
        return jnp.concatenate([v, v], 1)

    def power(i):
        for block in range(2):
            lane = pl.ds(256 * block, 256)
            gradient(i, lane)
            mix = cross[:, 256 * block : 256 * block + 256]
            k = kap[:, lane]
            k1 = k * grad[0]
            k2 = k * grad[1]
            flux[0] = k1 + mix * k2
            flux[1] = k2 + mix * k1
            flux[2] = k * grad[2]
            for h in range(2):
                rows = pl.ds(256 * h, 256)
                h2, l2 = cut(flux[1, rows])
                h3, l3 = cut(flux[2, rows])
                grad[0, rows] = dot(bwd_st[...], jnp.concatenate([h2, h3, h2, h3, l2, l3], 0))
            for q in range(2):
                part = jnp.concatenate([flux[0, pl.ds(64 * r + 32 * q, 32)] for r in range(8)], 0)
                high, low = cut(part)
                one = dot(bwd_r[...], jnp.concatenate([high, high, low], 0)).reshape(8, 32, 256)
                for r in range(8):
                    rows = pl.ds(64 * r + 32 * q, 32)
                    grad[0, rows] = grad[0, rows] + one[r]
            field = basis[i, :, :, :, lane].reshape(512, 256)
            value = grad[0] + volume2() * field
            basis[i + 1, :, :, :, lane] = value.reshape(8, 8, 8, 256)
            acc[2 * i + 1] += fold(value * field)

    def body(i, carry):
        power(i)
        assemble_start(i + 1)
        for block in range(2):
            norm(i, block)
        assemble_end(i + 1)
        return carry

    lax.fori_loop(0, ITERS - 1, body, 0)

    final = ITERS - 1
    for block in range(2):
        lane = pl.ds(256 * block, 256)
        norm(final, block)
        gradient(final, lane)
        mix = cross[:, 256 * block : 256 * block + 256]
        g1, g2, g3 = grad[0], grad[1], grad[2]
        field = basis[final, :, :, :, lane].reshape(512, 256)
        energy = kap[:, lane] * (g1 * g1 + g2 * g2 + g3 * g3 + 2.0 * mix * (g1 * g2))
        acc[2 * final + 1] += fold(energy + volume2() * (field * field))

    rows = jnp.concatenate([jnp.sum(acc[k], axis=0, keepdims=True) for k in range(16)], 0)
    mine = jnp.sum(rows, axis=1, keepdims=True)
    message = jnp.sum(jnp.where(iota((16, 128), 0) == iota((16, 128), 1), mine, 0.0), axis=0, keepdims=True)
    chan_sum[chan] = message
    copies = []
    for j in range(1, n_chan):
        copies.append(
            pltpu.make_async_remote_copy(
                src_ref=chan_sum.at[chan],
                dst_ref=chan_sum.at[chan],
                send_sem=chan_send.at[j],
                recv_sem=chan_recv.at[j],
                device_id=(slab, lax.rem(chan + j, n_chan)),
                device_id_type=MESH,
            )
        )
    for copy in copies:
        copy.start()
    for copy in copies:
        copy.wait()
    message = chan_sum[0]
    for j in range(1, n_chan):
        message = message + chan_sum[j]
    slab_sum[slab] = message
    copies = []
    for j in range(1, n_slab):
        copies.append(
            pltpu.make_async_remote_copy(
                src_ref=slab_sum.at[slab],
                dst_ref=slab_sum.at[slab],
                send_sem=slab_send.at[j],
                recv_sem=slab_recv.at[j],
                device_id=(lax.rem(slab + j, n_slab), chan),
                device_id_type=MESH,
            )
        )
    for copy in copies:
        copy.start()
    for copy in copies:
        copy.wait()
    message = slab_sum[0]
    for j in range(1, n_slab):
        message = message + slab_sum[j]
    lane1 = iota((1, 128), 1)
    moment = [
        jnp.sum(jnp.where(lane1 == k, message, 0.0), axis=1, keepdims=True) for k in range(2 * ITERS)
    ]
    weight = [w * (1.0 / SCALE) for w in krylov_weights(moment)]
    for l in range(2):
        for h in range(2):
            lane = pl.ds(256 * l + 128 * h, 128)
            total = weight[0] * basis[0, :, :, :, lane].reshape(512, 128)
            for i in range(1, ITERS):
                total = total + weight[i] * basis[i, :, :, :, lane].reshape(512, 128)
            out_ref[pl.ds(2 * h + l, 512, stride=4), :] = total


def panel(pack, prev, source, flags, plies, ops):
    n_slab, n_chan = lax.axis_size("slab"), lax.axis_size("chan")
    vmem = pl.BlockSpec(memory_space=pltpu.VMEM)
    dma = pltpu.SemaphoreType.DMA
    return pl.pallas_call(
        functools.partial(panel_kernel, n_slab, n_chan),
        in_specs=[vmem] * 10,
        out_specs=vmem,
        out_shape=jax.ShapeDtypeStruct((2048, 128), F32),
        scratch_shapes=[
            pltpu.VMEM((ITERS, 8, 8, 8, 512), F32),
            pltpu.VMEM((512, 512), F32),
            pltpu.VMEM((512, 512), F32),
            pltpu.VMEM((3, 512, 256), F32),
            pltpu.VMEM((3, 512, 256), F32),
            pltpu.VMEM((16, 8, 128), F32),
            pltpu.VMEM((3, 528, 128), BF16),
            pltpu.VMEM((ITERS, 2, 8, 128), F32),
            pltpu.VMEM((ITERS, 8, 8, 128), F32),
            pltpu.VMEM((ITERS, 2, 8, 8, 256), F32),
            pltpu.VMEM((ITERS, 2, 8, 8, 256), F32),
            pltpu.VMEM((n_chan, 1, 128), F32),
            pltpu.VMEM((n_slab, 1, 128), F32),
            dma((3,)),
            dma((3,)),
            dma((ITERS, 8)),
            dma((ITERS, 8)),
            dma((n_chan,)),
            dma((n_chan,)),
            dma((n_slab,)),
            dma((n_slab,)),
        ],
        compiler_params=pltpu.CompilerParams(collective_id=0, has_side_effects=True),
        name="panel",
    )(
        pack,
        prev,
        source,
        flags,
        plies,
        ops["fwd_st"],
        ops["fwd_r"],
        ops["bwd_st"],
        ops["bwd_r"],
        ops["volume"],
    )


def lanes_first(x):
    return x.reshape(512, 2, 2, 128).transpose(0, 2, 1, 3).reshape(2048, 128)


def on_device(u, index, prev, source, flags, plies):
    ops = operators()
    stepped, pack = fluid(u.reshape(192, 8, 512), index.reshape(1, 512), ops)
    warmth = panel(pack, lanes_first(prev), lanes_first(source), flags, plies, ops)
    warmth = warmth.reshape(512, 2, 2, 128).transpose(0, 2, 1, 3).reshape(8, 8, 8, 2, 256)
    return stepped.reshape(3, 8, 8, 8, 512), warmth


def solution(mesh):
    in_specs = (
        P(None, None, None, None, ("slab", "chan")),
        P(("slab", "chan")),
        P(None, None, None, "chan", "slab"),
        P(None, None, None, "chan", "slab"),
        P("chan", "slab"),
        P("chan", "slab"),
    )
    out_specs = (P(None, None, None, None, ("slab", "chan")), P(None, None, None, "chan", "slab"))
    return jax.shard_map(
        on_device, mesh=mesh, in_specs=in_specs, out_specs=out_specs, check_vma=False
    )
```

time: 1220 us -> 75.6 us (0.06)
  blocking collectives: 606 us -> 0 us
  local copies, waits for them, and re-layouts: 324 us -> 2.58 us
  matrix products: 106 us -> 0 us
  other arithmetic: 100 us -> 0 us
  Pallas kernels: 0 us -> 72.2 us
  starting transfers between devices: 52.3 us -> 0 us
  between operations: 13.9 us -> 0.64 us
    psum x9 -> x0, blocking collectives: 606 us -> none  [the longest x5 326 us: squared_norm(): lax.psum(jnp.sum(vector_field * vector_field * inv_mult), ('slab', 'chan'))]
    scatter x14 -> x0, local copies, waits for them, and re-layouts: 186 us -> none  [the longest x12 183 us: gather_nodes(): field = field.at[7, :, :, :, :-1].set(shared).at[0, :, :, :, 1:].set(shared)]
    dot_general x46 -> x0, matrix products: 106 us -> none  [the longest x25 45.1 us: backward(): jnp.einsum(backward_forms[conjugate_update_vector], matrix, field, precis...]
    scatter-add x13 -> x0, local copies, waits for them, and re-layouts: 92.8 us -> none  [gather_nodes(): field.at[0, :, :, :, 0].add(with_rims[0]).at[7, :, :, :, -1]]
    pallas_call x0 -> x2, Pallas kernels: none -> 72.2 us  [the longest x1 64.4 us: panel(): pl.pallas_call(functools.partial(panel_kernel, n_slab, n_chan), in_specs=...]
    ppermute x27 -> x0, starting transfers between devices: 52.3 us -> none  [the longest x12 28.4 us: with_halo(): before = lax.ppermute(last, axis, up)]
    add x32 -> x0, other arithmetic: 27.3 us -> none  [the longest x12 12.1 us: gather_nodes(): field.at[0, :, :, :, 0].add(with_rims[0]).at[7, :, :, :, -1]]
    another operation x11 -> x0, other arithmetic: 21 us -> none
  transfers between devices with their start and end apart: 27 -> 0, of which waited for: 6 -> 0; matrix products, arithmetic and copies ran while one was open for 26% -> 0% of each run, Pallas kernels for 0% -> 0%
where the time goes in v1:
time: 75.6 us; the launch traced here: 75.4 us
  Pallas kernels  72.2 us (96%)
  local copies, waits for them, and re-layouts  2.58 us (3%)
    pallas_call x1, Pallas kernels, panel(): pl.pallas_call(functools.partial(panel_kernel, n_slab, n_chan), in_specs=...  64.4 us
    pallas_call x1, Pallas kernels, fluid(): pl.pallas_call(fluid_kernel, grid=(blocks,), in_specs=[pl.BlockSpec((192,...  7.81 us
    unnamed x1, local copies, waits for them, and re-layouts  2.58 us

profile of v1, /device:TPU:0, one launch (start us, length us, event | category | flops | bytes accessed | tf_op | source)
XLA Modules:
  0.0 75.4 jit_solution(11644874349627757010)
XLA Ops:
  0.6 7.8 %fluid.1 = (bf16[192,8,512]{2,1,0:T(8,128)(2,1)}, bf16[5,528,128]{2,1,0:T(8,128)(2,1)}) custom-call(bf16[192,8,512]{2,1,0:T(8,128)(2,1)} %bitcast.19, s32[1,512]{1,0:T(1,128)} %bitcast.22, bf16[512,512]{1,0:T(8,128)(2,1)} %constant.22.clone.flu_st, bf16[256,512]{1,0:T(8,128)(2,1)} %constant.23.clone.flu_r, bf16[256,256]{1,0:T(8,128)(2,1)} %constant.24.clone.lap_st, ...), custom_call_target="tpu_custom_call" | custom-call | tf_op jit(solution)/shard_map/fluid/pallas_call | solution.py:180
  8.4 64.4 %panel.1 = f32[2048,128]{1,0:T(8,128)} custom-call(bf16[5,528,128]{2,1,0:T(8,128)(2,1)} %get-tuple-element.5.pack_ref, f32[2048,128]{1,0:T(8,128)} %bitcast.20, f32[2048,128]{1,0:T(8,128)} %bitcast.21, s32[2,256]{1,0:T(2,128)} %flag_ref.1, s32[2,256]{1,0:T(2,128)} %ply_ref.1, bf16[512,768]{1,0:T(8,128)(2,1)} %constant.18.clone.fwd_st, ...), custom_call_target="tpu_custom_call" | custom-call | tf_op jit(solution)/shard_map/panel/pallas_call | solution.py:596
  72.8 2.6 %copy.21 = f32[8,8,8,2,256]{4,3,2,1,0:T(2,128)} copy(f32[8,8,8,2,256]{4,3,2,1,0:T(2,128)} %bitcast.18) | data formatting | bytes 2097152

commit v2 on v1

--- a/solution.py
+++ b/solution.py
@@ -69,26 +69,17 @@
     along_r = kron(deriv, eye(32))
     ds_hi, ds_lo = two(along_s)
     dt_hi, dt_lo = two(along_t)
-    dr_hi, dr_lo = two(along_r)
-    fwd_st = np.block([[ds_hi, ds_lo, ds_hi], [dt_hi, dt_lo, dt_hi]])
-    fwd_r = np.block([[dr_hi, dr_lo, dr_hi]])
-    bwd_st = np.block([[ds_hi.T, dt_hi.T, ds_lo.T, dt_lo.T, ds_hi.T, dt_hi.T]])
-    bwd_r = np.block([[dr_hi.T, dr_lo.T, dr_hi.T]])
-    flu_st = np.block([[ds_hi, ds_lo], [dt_hi, dt_lo]])
-    flu_r = np.block([[dr_hi, dr_lo]])
+    forward = np.block([[ds_hi, ds_lo], [dt_hi, dt_lo]])
+    backward = np.block([[ds_hi.T, dt_hi.T, ds_lo.T, dt_lo.T]])
     lap_st = kron(eye(4), kron(second, eye(8))) + kron(eye(32), second)
-    lap_r = kron(second, eye(32))
+    both_r = np.block([[along_r], [kron(second, eye(32))]])
     volume = (weights[:, None, None] * weights[None, :, None] * weights[None, None, :]).reshape(512, 1)
     cast = lambda m: jnp.asarray(np.asarray(m, np.float32).astype(BF16))
     return {
-        "fwd_st": cast(fwd_st),
-        "fwd_r": cast(fwd_r),
-        "bwd_st": cast(bwd_st),
-        "bwd_r": cast(bwd_r),
-        "flu_st": cast(flu_st),
-        "flu_r": cast(flu_r),
+        "forward": cast(forward),
+        "backward": cast(backward),
         "lap_st": cast(lap_st),
-        "lap_r": cast(lap_r),
+        "both_r": cast(both_r),
         "volume": jnp.asarray(np.broadcast_to(volume, (512, 128)), F32),
     }
 
@@ -101,9 +92,7 @@
     return lax.broadcasted_iota(jnp.int32, shape, dim)
 
 
-def fluid_kernel(
-    u_ref, index_ref, flu_st, flu_r, lap_st, lap_r, out_ref, pack_ref, grad, lap, cond
-):
+def fluid_kernel(u_ref, index_ref, grad_st, lap_st, both_r, out_ref, pack_ref, grad, lap, cond):
     step = pl.program_id(0)
     lanes = u_ref.shape[2]
 
@@ -114,19 +103,18 @@
         for h in range(2):
             rows = pl.ds(256 * h, 256)
             part = low[256 * h : 256 * h + 256]
-            both = dot(flu_st[...], jnp.concatenate([part, part], 0))
+            both = dot(grad_st[...], part)
             grad[1, rows] = both[:256]
             grad[2, rows] = both[256:]
             lap[rows] = dot(lap_st[...], part)
         by_r = flat.reshape(8, 64, lanes)
         for q in range(2):
             part = by_r[:, 32 * q : 32 * q + 32].reshape(256, lanes).astype(BF16)
-            one = dot(flu_r[...], jnp.concatenate([part, part], 0)).reshape(8, 32, lanes)
-            more = dot(lap_r[...], part).reshape(8, 32, lanes)
+            both = dot(both_r[...], part).reshape(16, 32, lanes)
             for r in range(8):
                 rows = pl.ds(64 * r + 32 * q, 32)
-                grad[0, rows] = one[r]
-                lap[rows] = lap[rows] + more[r]
+                grad[0, rows] = both[r]
+                lap[rows] = lap[rows] + both[8 + r]
         u0 = u_ref[0:64].astype(F32).reshape(512, lanes)
         u1 = u_ref[64:128].astype(F32).reshape(512, lanes)
         u2 = u_ref[128:192].astype(F32).reshape(512, lanes)
@@ -183,10 +171,9 @@
         in_specs=[
             pl.BlockSpec((192, 8, lanes), lambda i: (0, 0, i)),
             fixed((1, 512)),
-            fixed((512, 512)),
-            fixed((256, 512)),
+            fixed((512, 256)),
             fixed((256, 256)),
-            fixed((256, 256)),
+            fixed((512, 256)),
         ],
         out_specs=[
             pl.BlockSpec((192, 8, lanes), lambda i: (0, 0, i)),
@@ -202,7 +189,7 @@
             pltpu.VMEM((528, 512), BF16),
         ],
         name="fluid",
-    )(u, index, ops["flu_st"], ops["flu_r"], ops["lap_st"], ops["lap_r"])
+    )(u, index, ops["forward"], ops["lap_st"], ops["both_r"])
 
 
 def krylov_weights(m):
@@ -243,15 +230,13 @@
     n_slab,
     n_chan,
     pack_ref,
-    prev_ref,
-    source_ref,
-    flag_ref,
-    ply_ref,
-    fwd_st,
-    fwd_r,
-    bwd_st,
-    bwd_r,
-    volume_ref,
+    prev_hbm,
+    source_hbm,
+    flag_hbm,
+    ply_hbm,
+    forward_ref,
+    backward_ref,
+    volume_hbm,
     out_ref,
     basis,
     kap,
@@ -266,6 +251,15 @@
     side_in,
     chan_sum,
     slab_sum,
+    prev_ref,
+    source_ref,
+    volume_ref,
+    flag_ref,
+    ply_ref,
+    own_pack,
+    fwd_st,
+    bwd_st,
+    load_sem,
     pack_send,
     pack_recv,
     halo_send,
@@ -289,6 +283,28 @@
     greet += [(lax.rem(slab + j, n_slab), chan) for j in range(2, n_slab - 1)]
     for peer in greet:
         pl.semaphore_signal(barrier, inc=1, device_id=peer, device_id_type=MESH)
+
+    loads = [
+        pltpu.make_async_copy(src, dst, load_sem.at[k])
+        for k, (src, dst) in enumerate(
+            (
+                (prev_hbm, prev_ref),
+                (source_hbm, source_ref),
+                (volume_hbm, volume_ref),
+                (flag_hbm, flag_ref),
+                (ply_hbm, ply_ref),
+                (pack_ref.at[pl.ds(0, 2)], own_pack),
+                (forward_ref, fwd_st.at[:, pl.ds(0, 512)]),
+                (forward_ref.at[:, pl.ds(0, 256)], fwd_st.at[:, pl.ds(512, 256)]),
+                (backward_ref, bwd_st.at[:, pl.ds(0, 1024)]),
+                (backward_ref.at[:, pl.ds(0, 512)], bwd_st.at[:, pl.ds(1024, 512)]),
+            )
+        )
+    ]
+    for load in loads:
+        load.start()
+    for load in loads[:5]:
+        load.wait()
 
     for l in range(2):
         for h in range(2):
@@ -312,30 +328,18 @@
     damping = jnp.where(flag == 1, 1.0 / (1.0 + 0.25 * ply), 1.0)
     cross = 0.4 * flag.astype(F32) * ply / (ply + 1.0)
 
-    pl.semaphore_wait(barrier, len(greet))
-
-    def device_at(step):
-        number = lax.rem(device + step + devices, devices)
-        return (number // n_chan, lax.rem(number, n_chan))
-
-    moves = []
-    for k, step in enumerate((1, -1, n_chan)):
-        copy = pltpu.make_async_remote_copy(
-            src_ref=pack_ref.at[2 + k],
-            dst_ref=got_pack.at[k],
-            send_sem=pack_send.at[k],
-            recv_sem=pack_recv.at[k],
-            device_id=device_at(step),
-            device_id_type=MESH,
-        )
-        copy.start()
-        moves.append(copy)
-
     lane8 = iota((8, 128), 1)
     has_left = slab > 0
     has_right = slab < n_slab - 1
     has_under = chan > 0
     has_over = chan < n_chan - 1
+
+    has_next = {(1, 0): has_right, (-1, 0): has_left, (0, 1): has_over, (0, -1): has_under}
+
+    def both_of(ds, dc):
+        if ds == 0 or dc == 0:
+            return has_next[ds, dc]
+        return has_next[ds, 0] & has_next[0, dc]
 
     def halo_copies(i):
         copies = []
@@ -373,7 +377,7 @@
         copies = halo_copies(i)
         for d, (ds, dc) in enumerate(HALO):
             if ds != 0:
-                copies[d].start()
+                pl.when(both_of(ds, dc))(copies[d].start)
         lane_a = iota((64, 256), 1)
         for l in range(2):
             lane = pl.ds(256 * l, 256)
@@ -389,15 +393,16 @@
         side_out[i, 1] = basis[i, :, 0, :, 0:256]
         for d, (ds, dc) in enumerate(HALO):
             if ds == 0:
-                copies[d].start()
+                pl.when(both_of(ds, dc))(copies[d].start)
         both = basis[i, :, 7, :, 0:256] + basis[i, :, 0, :, 256:512]
         basis[i, :, 7, :, 0:256] = both
         basis[i, :, 0, :, 256:512] = both
 
     def assemble_end(i):
         copies = halo_copies(i)
-        for copy in copies:
-            copy.wait()
+        for d, (ds, dc) in enumerate(HALO):
+            pl.when(both_of(ds, dc))(copies[d].wait_send)
+            pl.when(both_of(-ds, -dc))(copies[d].wait_recv)
         from_left = edge_in[i, 0]
         from_right = edge_in[i, 1]
         first = lane8 == 0
@@ -429,7 +434,25 @@
                 last & has_right & has, pltpu.roll(right, (127 - at) % 128, 1), 0.0
             )
 
+    pl.semaphore_wait(barrier, len(greet))
     assemble_start(0)
+
+    def device_at(step):
+        number = lax.rem(device + step + devices, devices)
+        return (number // n_chan, lax.rem(number, n_chan))
+
+    moves = []
+    for k, step in enumerate((1, -1, n_chan)):
+        copy = pltpu.make_async_remote_copy(
+            src_ref=pack_ref.at[2 + k],
+            dst_ref=got_pack.at[k],
+            send_sem=pack_send.at[k],
+            recv_sem=pack_recv.at[k],
+            device_id=device_at(step),
+            device_id_type=MESH,
+        )
+        copy.start()
+        moves.append(copy)
 
     def place(slots, block):
         code = block[512:528].astype(F32)
@@ -438,38 +461,58 @@
         value = dot(block[0:512], chosen, NT)
         return value if slots is None else slots + value
 
-    moved = place(place(None, pack_ref[0]), pack_ref[1])
-    for k in range(3):
-        moves[k].wait()
-        moved = place(moved, got_pack[k])
-    for h in range(4):
-        lane = pl.ds(128 * h, 128)
-        kap[:, lane] = (
-            volume_ref[...] * (1.0 / SCALE) * moved[:, 128 * h : 128 * h + 128] * damping[:, 128 * h : 128 * h + 128]
-        )
-
-    assemble_end(0)
+    loads[5].wait()
+    kap[...] = place(place(None, own_pack[0]), own_pack[1])
 
     def cut(x):
         high = x.astype(BF16)
         return high, (x - high.astype(F32)).astype(BF16)
 
-    def gradient(i, lane):
-        for h in range(2):
-            field = basis[i, 4 * h : 4 * h + 4, :, :, lane].reshape(256, 256)
-            high, low = cut(field)
-            both = dot(fwd_st[...], jnp.concatenate([high, high, low], 0))
-            grad[1, pl.ds(256 * h, 256)] = both[:256]
-            grad[2, pl.ds(256 * h, 256)] = both[256:]
-        for q in range(2):
-            field = basis[i, :, 4 * q : 4 * q + 4, :, lane].reshape(256, 256)
-            high, low = cut(field)
-            one = dot(fwd_r[...], jnp.concatenate([high, high, low], 0)).reshape(8, 32, 256)
-            for r in range(8):
-                grad[0, pl.ds(64 * r + 32 * q, 32)] = one[r]
+    def along_r(matrix, v):
+        even = [v[k] + v[7 - k] for k in range(4)]
+        odd = [v[k] - v[7 - k] for k in range(4)]
+        first, last = [], []
+        for i in range(4):
+            same = [0.5 * float(matrix[i, k] + matrix[i, 7 - k]) for k in range(4)]
+            flip = [0.5 * float(matrix[i, k] - matrix[i, 7 - k]) for k in range(4)]
+            p = (same[0] * even[0] + same[1] * even[1]) + (same[2] * even[2] + same[3] * even[3])
+            q = (flip[0] * odd[0] + flip[1] * odd[1]) + (flip[2] * odd[2] + flip[3] * odd[3])
+            first.append(p + q)
+            last.append(q - p)
+        return first + last[::-1]
+
+    deriv = gll()[0]
+
+    def gradient(i):
+        for block in range(2):
+            lane = pl.ds(256 * block, 256)
+            for h in range(2):
+                field = basis[i, 4 * h : 4 * h + 4, :, :, lane].reshape(256, 256)
+                high, low = cut(field)
+                both = dot(fwd_st[...], jnp.concatenate([high, high, low], 0))
+                grad[1, pl.ds(256 * h, 256), lane] = both[:256]
+                grad[2, pl.ds(256 * h, 256), lane] = both[256:]
+            for s in range(8):
+                for tile in range(2):
+                    part = pl.ds(256 * block + 128 * tile, 128)
+                    out = along_r(deriv, [basis[i, r, s, :, part] for r in range(8)])
+                    for r in range(8):
+                        grad[0, pl.ds(64 * r + 8 * s, 8), part] = out[r]
+
+    assemble_end(0)
+    for load in loads[6:]:
+        load.wait()
+    gradient(0)
+
+    for k in range(3):
+        moves[k].wait()
+        kap[...] = place(kap[...], got_pack[k])
+    for h in range(4):
+        lane = pl.ds(128 * h, 128)
+        kap[:, lane] = volume_ref[...] * (1.0 / SCALE) * kap[:, lane] * damping[:, 128 * h : 128 * h + 128]
 
     def fold(x):
-        total = jnp.sum(x.reshape(64, 8, 256), axis=0)
+        total = jnp.sum(x.reshape(x.shape[0] // 8, 8, 256), axis=0)
         return total[:, :128] + total[:, 128:]
 
     acc[...] = jnp.zeros_like(acc)
@@ -479,37 +522,32 @@
         field = basis[i, :, :, :, lane].reshape(512, 256)
         acc[2 * i] += fold(field * field * inv_mult[:, lane])
 
-    def volume2():
-        v = volume_ref[...] * (0.05 / SCALE)
-        return jnp.concatenate([v, v], 1)
-
     def power(i):
         for block in range(2):
             lane = pl.ds(256 * block, 256)
-            gradient(i, lane)
             mix = cross[:, 256 * block : 256 * block + 256]
             k = kap[:, lane]
-            k1 = k * grad[0]
-            k2 = k * grad[1]
+            k1 = k * grad[0, :, lane]
+            k2 = k * grad[1, :, lane]
             flux[0] = k1 + mix * k2
             flux[1] = k2 + mix * k1
-            flux[2] = k * grad[2]
+            flux[2] = k * grad[2, :, lane]
+            for s in range(8):
+                for tile in range(2):
+                    part = pl.ds(128 * tile, 128)
+                    out = along_r(deriv.T, [flux[0, pl.ds(64 * r + 8 * s, 8), part] for r in range(8)])
+                    for r in range(8):
+                        flux[0, pl.ds(64 * r + 8 * s, 8), part] = out[r]
             for h in range(2):
                 rows = pl.ds(256 * h, 256)
                 h2, l2 = cut(flux[1, rows])
                 h3, l3 = cut(flux[2, rows])
-                grad[0, rows] = dot(bwd_st[...], jnp.concatenate([h2, h3, h2, h3, l2, l3], 0))
-            for q in range(2):
-                part = jnp.concatenate([flux[0, pl.ds(64 * r + 32 * q, 32)] for r in range(8)], 0)
-                high, low = cut(part)
-                one = dot(bwd_r[...], jnp.concatenate([high, high, low], 0)).reshape(8, 32, 256)
-                for r in range(8):
-                    rows = pl.ds(64 * r + 32 * q, 32)
-                    grad[0, rows] = grad[0, rows] + one[r]
-            field = basis[i, :, :, :, lane].reshape(512, 256)
-            value = grad[0] + volume2() * field
-            basis[i + 1, :, :, :, lane] = value.reshape(8, 8, 8, 256)
-            acc[2 * i + 1] += fold(value * field)
+                value = dot(bwd_st[...], jnp.concatenate([h2, h3, h2, h3, l2, l3], 0))
+                field = basis[i, 4 * h : 4 * h + 4, :, :, lane].reshape(256, 256)
+                v = volume_ref[rows] * (0.05 / SCALE)
+                value = value + flux[0, rows] + jnp.concatenate([v, v], 1) * field
+                basis[i + 1, 4 * h : 4 * h + 4, :, :, lane] = value.reshape(4, 8, 8, 256)
+                acc[2 * i + 1] += fold(value * field)
 
     def body(i, carry):
         power(i)
@@ -517,6 +555,7 @@
         for block in range(2):
             norm(i, block)
         assemble_end(i + 1)
+        gradient(i + 1)
         return carry
 
     lax.fori_loop(0, ITERS - 1, body, 0)
@@ -525,12 +564,14 @@
     for block in range(2):
         lane = pl.ds(256 * block, 256)
         norm(final, block)
-        gradient(final, lane)
-        mix = cross[:, 256 * block : 256 * block + 256]
-        g1, g2, g3 = grad[0], grad[1], grad[2]
-        field = basis[final, :, :, :, lane].reshape(512, 256)
-        energy = kap[:, lane] * (g1 * g1 + g2 * g2 + g3 * g3 + 2.0 * mix * (g1 * g2))
-        acc[2 * final + 1] += fold(energy + volume2() * (field * field))
+        mix = 2.0 * cross[:, 256 * block : 256 * block + 256]
+        for h in range(4):
+            rows = pl.ds(128 * h, 128)
+            g1, g2, g3 = grad[0, rows, lane], grad[1, rows, lane], grad[2, rows, lane]
+            field = basis[final, 2 * h : 2 * h + 2, :, :, lane].reshape(128, 256)
+            v = volume_ref[rows] * (0.05 / SCALE)
+            energy = kap[rows, lane] * (g1 * (g1 + mix * g2) + g2 * g2 + g3 * g3)
+            acc[2 * final + 1] += fold(energy + jnp.concatenate([v, v], 1) * (field * field))
 
     rows = jnp.concatenate([jnp.sum(acc[k], axis=0, keepdims=True) for k in range(16)], 0)
     mine = jnp.sum(rows, axis=1, keepdims=True)
@@ -580,29 +621,33 @@
         jnp.sum(jnp.where(lane1 == k, message, 0.0), axis=1, keepdims=True) for k in range(2 * ITERS)
     ]
     weight = [w * (1.0 / SCALE) for w in krylov_weights(moment)]
-    for l in range(2):
-        for h in range(2):
-            lane = pl.ds(256 * l + 128 * h, 128)
-            total = weight[0] * basis[0, :, :, :, lane].reshape(512, 128)
-            for i in range(1, ITERS):
-                total = total + weight[i] * basis[i, :, :, :, lane].reshape(512, 128)
-            out_ref[pl.ds(2 * h + l, 512, stride=4), :] = total
+    full = [jnp.broadcast_to(w, (8, 128)) for w in weight]
+    for r in range(8):
+        for s in range(8):
+            for l in range(2):
+                for h in range(2):
+                    lane = pl.ds(256 * l + 128 * h, 128)
+                    total = full[0] * basis[0, r, s, :, lane]
+                    for i in range(1, ITERS):
+                        total = total + full[i] * basis[i, r, s, :, lane]
+                    out_ref[pl.ds(256 * r + 32 * s + 2 * h + l, 8, stride=4), :] = total
 
 
 def panel(pack, prev, source, flags, plies, ops):
     n_slab, n_chan = lax.axis_size("slab"), lax.axis_size("chan")
     vmem = pl.BlockSpec(memory_space=pltpu.VMEM)
+    anywhere = pl.BlockSpec(memory_space=pl.ANY)
     dma = pltpu.SemaphoreType.DMA
     return pl.pallas_call(
         functools.partial(panel_kernel, n_slab, n_chan),
-        in_specs=[vmem] * 10,
+        in_specs=[anywhere] * 8,
         out_specs=vmem,
         out_shape=jax.ShapeDtypeStruct((2048, 128), F32),
         scratch_shapes=[
             pltpu.VMEM((ITERS, 8, 8, 8, 512), F32),
             pltpu.VMEM((512, 512), F32),
             pltpu.VMEM((512, 512), F32),
-            pltpu.VMEM((3, 512, 256), F32),
+            pltpu.VMEM((3, 512, 512), F32),
             pltpu.VMEM((3, 512, 256), F32),
             pltpu.VMEM((16, 8, 128), F32),
             pltpu.VMEM((3, 528, 128), BF16),
@@ -612,6 +657,15 @@
             pltpu.VMEM((ITERS, 2, 8, 8, 256), F32),
             pltpu.VMEM((n_chan, 1, 128), F32),
             pltpu.VMEM((n_slab, 1, 128), F32),
+            pltpu.VMEM((2048, 128), F32),
+            pltpu.VMEM((2048, 128), F32),
+            pltpu.VMEM((512, 128), F32),
+            pltpu.VMEM((2, 256), jnp.int32),
+            pltpu.VMEM((2, 256), jnp.int32),
+            pltpu.VMEM((2, 528, 128), BF16),
+            pltpu.VMEM((512, 768), BF16),
+            pltpu.VMEM((256, 1536), BF16),
+            dma((10,)),
             dma((3,)),
             dma((3,)),
             dma((ITERS, 8)),
@@ -629,10 +683,8 @@
         source,
         flags,
         plies,
-        ops["fwd_st"],
-        ops["fwd_r"],
-        ops["bwd_st"],
-        ops["bwd_r"],
+        ops["forward"],
+        ops["backward"],
         ops["volume"],
     )
 

time: 75.6 us -> 61.4 us (0.81)
  Pallas kernels: 72.2 us -> 58 us
    pallas_call x1, Pallas kernels: 64.4 us -> 51.8 us  [panel(): pl.pallas_call(functools.partial(panel_kernel, n_slab, n_chan), in_specs=...]
    pallas_call x1, Pallas kernels: 7.81 us -> 6.24 us  [fluid(): pl.pallas_call(fluid_kernel, grid=(blocks,), in_specs=[pl.BlockSpec((192,...]
where the time goes in v2:
time: 61.4 us; the launch traced here: 61.2 us
  Pallas kernels  58 us (94%)
  local copies, waits for them, and re-layouts  2.58 us (4%)
  between operations  0.64 us (1%)
    pallas_call x1, Pallas kernels, panel(): pl.pallas_call(functools.partial(panel_kernel, n_slab, n_chan), in_specs=...  51.8 us
    pallas_call x1, Pallas kernels, fluid(): pl.pallas_call(fluid_kernel, grid=(blocks,), in_specs=[pl.BlockSpec((192,...  6.24 us
    unnamed x1, local copies, waits for them, and re-layouts  2.58 us

profile of v2, /device:TPU:0, one launch (start us, length us, event | category | flops | bytes accessed | tf_op | source)
XLA Modules:
  0.0 61.2 jit_solution(16505539280907360620)
XLA Ops:
  0.6 6.2 %fluid.1 = (bf16[192,8,512]{2,1,0:T(8,128)(2,1)}, bf16[5,528,128]{2,1,0:T(8,128)(2,1)}) custom-call(bf16[192,8,512]{2,1,0:T(8,128)(2,1)} %bitcast.19, s32[1,512]{1,0:T(1,128)} %bitcast.22, bf16[512,512]{1,0:T(8,128)(2,1)} %constant.10.clone.grad_st.forward_ref, bf16[256,256]{1,0:T(8,128)(2,1)} %constant.12.clone.lap_st, bf16[512,256]{1,0:T(8,128)(2,1)} %constant.13.clone.both_r), custom_call_target="tpu_custom_call" | custom-call | tf_op jit(solution)/shard_map/fluid/pallas_call | solution.py:168
  6.9 51.8 %panel.1 = f32[2048,128]{1,0:T(8,128)} custom-call(bf16[5,528,128]{2,1,0:T(8,128)(2,1)} %get-tuple-element.5.pack_ref, f32[2048,128]{1,0:T(8,128)} %bitcast.20, f32[2048,128]{1,0:T(8,128)} %bitcast.21, s32[2,256]{1,0:T(2,128)} %flag_hbm.1, s32[2,256]{1,0:T(2,128)} %ply_hbm.1, bf16[512,512]{1,0:T(8,128)(2,1)} %constant.10.clone.grad_st.forward_ref, ...), custom_call_target="tpu_custom_call" | custom-call | tf_op jit(solution)/shard_map/panel/pallas_call | solution.py:641
  58.7 2.6 %copy.17 = f32[8,8,8,2,256]{4,3,2,1,0:T(2,128)} copy(f32[8,8,8,2,256]{4,3,2,1,0:T(2,128)} %bitcast.18) | data formatting | bytes 2097152
